TPU v7x, 32 devices: a whole 2x2x4 slice. The times are simulated.
32 devices in a mesh: pipe: 8 (over z, y), dp: 4 (over x, core).
Axes of the slice: x: 2, y: 2, z: 4, core: 2. Of those that a mesh axis runs over, the one named last changes fastest.
Arguments:
- grad_output: bfloat16 [512, 8192], P('dp'), may hold values from -6 to 6
- hidden: bfloat16 [512, 14336], P('dp', 'pipe'), may hold values from -6 to 6
- next_hidden: bfloat16 [512, 14336], P('dp', 'pipe'), may hold values from -6 to 6
- master: float32 [14336, 8192], P('pipe', 'dp'), may hold values from -0.046875 to 0.046875
- moment: float32 [14336, 8192], P('pipe', 'dp'), may hold values from -24 to 24
- second_moment: float32 [14336, 8192], P('pipe', 'dp'), may hold values from 5 to 100
Outputs:
- update: float32 [14336, 8192], P('pipe', 'dp')
- upstream_grad: bfloat16 [512, 14336], P('dp', 'pipe')
- next_output: bfloat16 [512, 8192], P('pipe', 'dp')
All inputs are finite; a program needn't handle non-finite values.
Results may differ from a plain program's by a relative error of at most 0.005.
Values may be sent and summed in bfloat16 or wider, within the bound.
A program may use at most 256 MiB of HBM per device.

v0:
```python
import jax
import jax.numpy as jnp
from jax import lax
from jax.sharding import PartitionSpec as P

beta_one = 0.9
beta_two = 0.95
corr_one = 1.0 - 0.9**10
corr_two = 1.0 - 0.95**10
learn_rate = 0.005
decay_rate = 0.1
epsilon = 1e-08


def on_device(grad_output, hidden, next_hidden, master, moment, second_moment):
    weights_low = master.astype(jnp.bfloat16)
    columns = lax.all_to_all(grad_output, "dp", split_axis=1, concat_axis=0, tiled=True)
    rows_part = columns
    hidden_sum = lax.psum_scatter(
        lax.dot_general(
            rows_part, weights_low, (((1,), (1,)), ((), ())), preferred_element_type=jnp.float32
        ),
        "dp",
        scatter_dimension=0,
        tiled=True,
    )
    upstream = hidden_sum.astype(jnp.bfloat16)
    gathered = lax.all_gather(hidden, "dp", axis=0, tiled=True)
    gradient = lax.dot_general(
        gathered, columns, (((0,), (0,)), ((), ())), preferred_element_type=jnp.float32
    )
    moment_new = beta_one * moment + (1.0 - beta_one) * gradient
    second_new = beta_two * second_moment + (1.0 - beta_two) * gradient * gradient
    update = -(
        moment_new / corr_one / (jnp.sqrt(second_new / corr_two) + epsilon) + decay_rate * master
    )
    fresh_low = (master + learn_rate * update).astype(jnp.bfloat16)
    later_rows = lax.all_gather(next_hidden, "dp", axis=0, tiled=True)
    rows_part = later_rows
    next_out = lax.psum_scatter(
        jnp.dot(rows_part, fresh_low, preferred_element_type=jnp.float32),
        "pipe",
        scatter_dimension=0,
        tiled=True,
    ).astype(jnp.bfloat16)
    return (update, upstream, next_out)


def solution(mesh):
    in_specs = (
        P("dp", None),
        P("dp", "pipe"),
        P("dp", "pipe"),
        P("pipe", "dp"),
        P("pipe", "dp"),
        P("pipe", "dp"),
    )
    out_specs = (P("pipe", "dp"), P("dp", "pipe"), P("pipe", "dp"))
    return jax.shard_map(
        on_device, mesh=mesh, in_specs=in_specs, out_specs=out_specs, check_vma=False
    )
```

profile of v0, /device:TPU:0, one launch (start us, length us, event | category | flops | bytes accessed | tf_op | source)
XLA Modules:
  0.0 211.2 jit_solution(2200444903130895348)
XLA Ops:
  7.2 0.0 all-gather.3.cloned.1.call-start
  7.2 0.7 all-gather.3.cloned.1.call-update
  7.9 4.1 %copy.14 = bf16[128,8192]{0,1:T(8,128)(2,1)} copy(bf16[128,8192]{1,0:T(8,128)(2,1)} %param.6) | data formatting | bytes 4194304 | tf_op args[0]
  12.0 4.2 %all-to-all-start = ((bf16[128,4,2048]{0,2,1:T(8,128)(2,1)}), bf16[128,4,2048]{0,2,1:T(8,128)(2,1)S(1)}, u32[]{:S(2)}, u32[]{:S(2)}) async-start(bf16[128,4,2048]{0,2,1:T(8,128)(2,1)} %bitcast.11), calls=%async_computation | async-start | bytes 4194304 | tf_op jit(solution)/shard_map/all_to_all | solution.py:17
  16.2 0.0 all-gather.5.cloned.1.call-start
  16.2 0.7 all-gather.5.cloned.1.call-update
  16.9 0.0 reduce-scatter.5.cloned.1.call-start
  17.0 34.7 %all-to-all-done = bf16[128,4,2048]{0,2,1:T(8,128)(2,1)S(1)} async-done(((bf16[128,4,2048]{0,2,1:T(8,128)(2,1)}), bf16[128,4,2048]{0,2,1:T(8,128)(2,1)S(1)}, u32[]{:S(2)}, u32[]{:S(2)}) %all-to-all-start) | async-done | bytes 2097184 | tf_op jit(solution)/shard_map/all_to_all | solution.py:17
  51.7 2.6 %copy.15 = bf16[4,128,2048]{2,1,0:T(8,128)(2,1)} copy(bf16[4,128,2048]{1,2,0:T(8,128)(2,1)S(1)} %bitcast.10) | data formatting | bytes 4194304 | tf_op jit(solution)/shard_map/all_to_all | solution.py:17
  54.3 0.0 copy-start
  54.3 11.8 %fusion.9 = f32[512,1792]{1,0:T(8,128)} fusion(bf16[512,2048]{1,0:T(8,128)(2,1)} %bitcast.12, f32[1792,2048]{1,0:T(8,128)} %param.9), kind=kOutput, calls=%fused_computation.11 | convolution fusion | flops 3761766400 | bytes 20447232 | tf_op jit(solution)/shard_map/dot_general | solution.py:20
  66.1 0.0 reduce-scatter.5.cloned.1.call-update
  66.1 0.2 reduce-scatter.7.cloned.1.call-start
  66.4 0.0 all-gather.3.cloned.1.call-done
  66.4 0.0 copy-done
  66.4 25.2 %fusion.6 = f32[1792,2048]{1,0:T(8,128)} fusion(f32[1792,2048]{1,0:T(8,128)} %param.9, f32[1792,2048]{1,0:T(8,128)} %param.11, f32[1792,2048]{1,0:T(8,128)} %param.10, bf16[512,1792]{1,0:T(8,128)(2,1)} %all-gather.3.cloned.1.call-done, bf16[512,2048]{1,0:T(8,128)(2,1)S(1)} %bitcast.13), kind=kOutput, calls=%fused_computation.8 | convolution fusion | flops 3809476608 | bytes 62652416 | tf_op jit(solution)/shard_map/dot_general | solution.py:29
  91.6 0.0 all-gather.5.cloned.1.call-done
  91.6 16.1 %fusion.11 = f32[512,2048]{0,1:T(8,128)} fusion(bf16[512,1792]{1,0:T(8,128)(2,1)} %all-gather.5.cloned.1.call-done, f32[1792,2048]{1,0:T(8,128)} %param.9, f32[1792,2048]{1,0:T(8,128)} %fusion.6), kind=kOutput, calls=%fused_computation.13 | convolution fusion | flops 3769106432 | bytes 35389440 | tf_op jit(solution)/shard_map/dot_general | solution.py:41
  107.8 5.5 %copy.17 = f32[512,2048]{1,0:T(8,128)} copy(f32[512,2048]{0,1:T(8,128)} %fusion.11) | data formatting | bytes 8388608
  113.2 0.0 reduce-scatter.7.cloned.1.call-update
  113.2 0.0 reduce-scatter.5.cloned.1.call-done
  113.3 2.0 convert_element_type.13
  115.3 87.2 %reduce-scatter.7.cloned.1.call-done = f32[64,2048]{1,0:T(8,128)} async-done(((f32[512,2048]{1,0:T(8,128)}), f32[64,2048]{1,0:T(8,128)}) %reduce-scatter.7.cloned.1.call-update) | async-done | bytes 524304
  202.5 1.3 copy.18
  203.8 0.9 copy.16
Async XLA Ops:
  7.2 59.2 %all-gather.3.cloned.1.call-start = ((), (), s32[]{:S(2)}) async-start(), calls=%async_computation.3 | async-start | bytes 2293760 | tf_op jit(solution)/shard_map/all_gather | solution.py:28
  12.0 39.7 %all-to-all-start = ((bf16[128,4,2048]{0,2,1:T(8,128)(2,1)}), bf16[128,4,2048]{0,2,1:T(8,128)(2,1)S(1)}, u32[]{:S(2)}, u32[]{:S(2)}) async-start(bf16[128,4,2048]{0,2,1:T(8,128)(2,1)} %bitcast.11), calls=%async_computation | async-start | bytes 4194304 | tf_op jit(solution)/shard_map/all_to_all | solution.py:17
  16.2 75.4 %all-gather.5.cloned.1.call-start = ((), (), s32[]{:S(2)}) async-start(), calls=%async_computation.5 | async-start | bytes 2293760 | tf_op jit(solution)/shard_map/all_gather | solution.py:38
  16.9 96.4 %reduce-scatter.5.cloned.1.call-start = ((), (), s32[]{:S(2)}) async-start(), calls=%async_computation.4 | async-start | bytes 4587520 | tf_op jit(solution)/shard_map/reduce_scatter | solution.py:19
  54.3 12.1 %copy-start = (bf16[4,128,2048]{2,1,0:T(8,128)(2,1)S(1)}, bf16[4,128,2048]{2,1,0:T(8,128)(2,1)}, u32[]{:S(2)}) copy-start(bf16[4,128,2048]{2,1,0:T(8,128)(2,1)} %copy.15) | copy-start | bytes 6291460
  66.1 136.3 %reduce-scatter.7.cloned.1.call-start = ((), (), s32[]{:S(2)}) async-start(), calls=%async_computation.6 | async-start | bytes 4718592
Sparse Core Ops, SparseCore 0:
  9.6 33.7 all-gather.2
  44.9 21.0 all-gather.4
  68.6 41.2 reduce-scatter.4
  113.8 88.6 reduce-scatter.6
where the time goes:
time: 212 us; the launch traced here: 211 us
  waiting for transfers between devices  123 us (58%)
  matrix products  53.2 us (25%)
  local copies, waits for them, and re-layouts  14.3 us (7%)
  between operations  13.8 us (7%)
  starting transfers between devices  4.51 us (2%)
    unnamed x5, waiting for transfers between devices  88.6 us
    all_to_all x1, waiting for transfers between devices, on_device(): lax.all_to_all(grad_output, 'dp', split_axis=1, concat_axis=0, tiled=True)  34.7 us
    dot_general x1, matrix products, on_device(): lax.dot_general(gathered, columns, (((0,), (0,)), ((), ())), preferred_el...  25.2 us
    dot_general x1, matrix products, on_device(): jnp.dot(rows_part, fresh_low, preferred_element_type=jnp.float32)  16.1 us
    dot_general x1, matrix products, on_device(): lax.dot_general(rows_part, weights_low, (((1,), (1,)), ((), ())), preferr...  11.8 us
    unnamed x6, local copies, waits for them, and re-layouts  11.8 us
  transfers between devices with their start and end apart: 5, of which 2 were waited for; matrix products, arithmetic and copies ran while one was open for 32% of the time, Pallas kernels for 0%

commit v1 on v0

--- a/solution.py
+++ b/solution.py
@@ -12,9 +12,25 @@
 epsilon = 1e-08
 
 
+def swapped_with_each(x, axis, split, join):
+    ways, here = (lax.axis_size(axis), lax.axis_index(axis))
+    width = x.shape[split] // ways
+    lengths = list(x.shape)
+    lengths[split] = width
+    height = lengths[join]
+    lengths[join] = height * ways
+    full = jnp.zeros(lengths, x.dtype)
+    for mask in range(ways):
+        part = lax.dynamic_slice_in_dim(x, (here ^ mask) * width, width, axis=split)
+        if mask:
+            part = lax.ppermute(part, axis, [(d, d ^ mask) for d in range(ways)])
+        full = lax.dynamic_update_slice_in_dim(full, part, (here ^ mask) * height, axis=join)
+    return full
+
+
 def on_device(grad_output, hidden, next_hidden, master, moment, second_moment):
     weights_low = master.astype(jnp.bfloat16)
-    columns = lax.all_to_all(grad_output, "dp", split_axis=1, concat_axis=0, tiled=True)
+    columns = swapped_with_each(grad_output, "dp", 1, 0)
     rows_part = columns
     hidden_sum = lax.psum_scatter(
         lax.dot_general(

time: 212 us -> 247 us (1.17)
  local copies, waits for them, and re-layouts: 14.3 us -> 70.2 us
  waiting for transfers between devices: 123 us -> 106 us
  matrix products: 53.2 us -> 50.7 us
    unnamed x6 -> x7, local copies, waits for them, and re-layouts: 11.8 us -> 66 us
    all_to_all x1 -> x0, waiting for transfers between devices: 34.7 us -> none  [on_device(): lax.all_to_all(grad_output, 'dp', split_axis=1, concat_axis=0, tiled=True)]
    ppermute x0 -> x3, waiting for transfers between devices: none -> 32.4 us  [swapped_with_each(): part = lax.ppermute(part, axis, [(d, d ^ mask) for d in range(ways)])]
    unnamed x5, waiting for transfers between devices: 88.6 us -> 73.8 us
    all_to_all x1 -> x0, starting transfers between devices: 4.21 us -> none  [on_device(): lax.all_to_all(grad_output, 'dp', split_axis=1, concat_axis=0, tiled=True)]
    ppermute x0 -> x3, starting transfers between devices: none -> 3.09 us  [swapped_with_each(): part = lax.ppermute(part, axis, [(d, d ^ mask) for d in range(ways)])]
    dynamic_slice x0 -> x1, local copies, waits for them, and re-layouts: none -> 2.75 us  [swapped_with_each(): part = lax.dynamic_slice_in_dim(x, (here ^ mask) * width, width, axis=split)]
    all_to_all x1 -> x0, local copies, waits for them, and re-layouts: 2.58 us -> none  [on_device(): lax.all_to_all(grad_output, 'dp', split_axis=1, concat_axis=0, tiled=True)]
  transfers between devices with their start and end apart: 5 -> 7, of which waited for: 2 -> 3; matrix products, arithmetic and copies ran while one was open for 32% -> 49% of each run, Pallas kernels for 0% -> 0%
where the time goes in v1:
time: 247 us; the launch traced here: 246 us
  waiting for transfers between devices  106 us (43%)
  local copies, waits for them, and re-layouts  70.2 us (28%)
  matrix products  50.7 us (21%)
  between operations  13.8 us (6%)
  starting transfers between devices  3.42 us (1%)
    unnamed x5, waiting for transfers between devices  73.8 us
    unnamed x7, local copies, waits for them, and re-layouts  66 us
    ppermute x3, waiting for transfers between devices, swapped_with_each(): part = lax.ppermute(part, axis, [(d, d ^ mask) for d in range(ways)])  32.4 us
    dot_general x1, matrix products, on_device(): lax.dot_general(gathered, columns, (((0,), (0,)), ((), ())), preferred_el...  25.2 us
    dot_general x1, matrix products, on_device(): jnp.dot(rows_part, fresh_low, preferred_element_type=jnp.float32)  15.8 us
    dot_general x1, matrix products, on_device(): lax.dot_general(rows_part, weights_low, (((1,), (1,)), ((), ())), preferr...  9.69 us
  transfers between devices with their start and end apart: 7, of which 3 were waited for; matrix products, arithmetic and copies ran while one was open for 49% of the time, Pallas kernels for 0%

profile of v1, /device:TPU:0, one launch (start us, length us, event | category | flops | bytes accessed | tf_op | source)
XLA Modules:
  0.0 246.3 jit_solution(3590247845730653552)
XLA Ops:
  7.2 0.0 all-gather.3.cloned.1.call-start
  7.2 0.7 all-gather.3.cloned.1.call-update
  7.9 0.0 all-gather.5.cloned.1.call-start
  7.9 0.7 all-gather.5.cloned.1.call-update
  8.6 0.0 reduce-scatter.5.cloned.1.call-start
  8.7 0.2 broadcast_in_dim.3
  9.0 2.7 %constant_dynamic-slice_fusion = (bf16[128,2048]{1,0:T(8,128)(2,1)}, bf16[128,2048]{1,0:T(8,128)(2,1)}, bf16[512,2048]{1,0:T(8,128)(2,1)S(1)}, bf16[128,2048]{1,0:T(8,128)(2,1)}) fusion(bf16[128,8192]{1,0:T(8,128)(2,1)} %param.6, s32[]{:T(128)S(6)} %select_n.30, s32[]{:T(128)S(6)} %select_n.26, bf16[512,2048]{1,0:T(8,128)(2,1)S(1)} %broadcast_in_dim.3, ...), kind=kLoop, calls=%fused_computation.18 | loop fusion | bytes 4194324 | tf_op jit(solution)/shard_map/dynamic_slice | solution.py:24
  11.7 0.5 collective-permute-start
  12.2 2.5 %collective-permute-start.1 = (bf16[128,2048]{1,0:T(8,128)(2,1)}, bf16[128,2048]{1,0:T(8,128)(2,1)S(1)}, u32[]{:S(2)}, u32[]{:S(2)}) collective-permute-start(bf16[128,2048]{1,0:T(8,128)(2,1)} %get-tuple-element.12), channel_id=1, source_target_pairs={{0,2},{1,3},{2,0},{3,1},{4,6},{5,7},{6,4},{7,5},{8,10},{9,11},{10,... | collective-permute-start | bytes 1572872 | tf_op jit(solution)/shard_map/ppermute | solution.py:26
  14.7 0.1 collective-permute-start.2
  14.8 0.0 collective-permute-done
  14.8 1.1 constant_dynamic-update-slice_fusion.1
  15.9 18.4 %collective-permute-done.1 = bf16[128,2048]{1,0:T(8,128)(2,1)S(1)} collective-permute-done((bf16[128,2048]{1,0:T(8,128)(2,1)}, bf16[128,2048]{1,0:T(8,128)(2,1)S(1)}, u32[]{:S(2)}, u32[]{:S(2)}) %collective-permute-start.1) | collective-permute-done | bytes 524320 | tf_op jit(solution)/shard_map/ppermute | solution.py:26
  34.3 14.0 %collective-permute-done.2 = bf16[128,2048]{1,0:T(8,128)(2,1)S(1)} collective-permute-done((bf16[128,2048]{1,0:T(8,128)(2,1)}, bf16[128,2048]{1,0:T(8,128)(2,1)S(1)}, u32[]{:S(2)}, u32[]{:S(2)}) %collective-permute-start.2) | collective-permute-done | bytes 524320 | tf_op jit(solution)/shard_map/ppermute | solution.py:26
  48.4 9.7 %fusion.11 = f32[512,1792]{1,0:T(8,128)} fusion(bf16[512,2048]{1,0:T(8,128)(2,1)S(1)} %constant_dynamic-update-slice_fusion.2, f32[1792,2048]{1,0:T(8,128)} %param.9), kind=kOutput, calls=%fused_computation.14 | convolution fusion | flops 3761766400 | bytes 20447232 | tf_op jit(solution)/shard_map/dot_general | solution.py:36
  58.1 0.0 reduce-scatter.5.cloned.1.call-update
  58.1 0.2 reduce-scatter.7.cloned.1.call-start
  58.3 14.3 %copy.17 = f32[1792,2048]{0,1:T(8,128)} copy(f32[1792,2048]{1,0:T(8,128)} %param.9) | data formatting | bytes 29360128 | tf_op args[3]
  72.6 14.5 %copy.15 = f32[1792,2048]{0,1:T(8,128)} copy(f32[1792,2048]{1,0:T(8,128)} %param.10) | data formatting | bytes 29360128 | tf_op args[4]
  87.1 14.4 %copy.16 = f32[1792,2048]{0,1:T(8,128)} copy(f32[1792,2048]{1,0:T(8,128)} %param.11) | data formatting | bytes 29360128 | tf_op args[5]
  101.5 0.0 all-gather.3.cloned.1.call-done
  101.5 25.2 %fusion.8 = f32[1792,2048]{0,1:T(8,128)} fusion(f32[1792,2048]{0,1:T(8,128)} %copy.17, f32[1792,2048]{0,1:T(8,128)} %copy.16, f32[1792,2048]{0,1:T(8,128)} %copy.15, bf16[512,2048]{1,0:T(8,128)(2,1)S(1)} %constant_dynamic-update-slice_fusion.2, bf16[512,1792]{1,0:T(8,128)(2,1)} %all-gather.3.cloned.1.call-done), kind=kOutput, calls=%fused_computation.11 | convolution fusion | flops 3809476608 | bytes 62652416 | tf_op jit(solution)/shard_map/dot_general | solution.py:45
  126.7 0.0 all-gather.5.cloned.1.call-done
  126.7 15.8 %fusion.13 = f32[512,2048]{0,1:T(8,128)} fusion(bf16[512,1792]{1,0:T(8,128)(2,1)} %all-gather.5.cloned.1.call-done, f32[1792,2048]{0,1:T(8,128)} %copy.17, f32[1792,2048]{0,1:T(8,128)} %fusion.8), kind=kOutput, calls=%fused_computation.16 | convolution fusion | flops 3769106432 | bytes 35389440 | tf_op jit(solution)/shard_map/dot_general | solution.py:57
  142.5 5.4 %copy.21 = f32[512,2048]{1,0:T(8,128)} copy(f32[512,2048]{0,1:T(8,128)} %fusion.13) | data formatting | bytes 8388608
  147.9 0.0 reduce-scatter.7.cloned.1.call-update
  147.9 15.2 %copy.19 = f32[1792,2048]{1,0:T(8,128)} copy(f32[1792,2048]{0,1:T(8,128)} %fusion.8) | data formatting | bytes 29360128
  163.2 0.0 reduce-scatter.5.cloned.1.call-done
  163.2 2.0 convert_element_type.13
  165.2 72.4 %reduce-scatter.7.cloned.1.call-done = f32[64,2048]{1,0:T(8,128)} async-done(((f32[512,2048]{1,0:T(8,128)}), f32[64,2048]{1,0:T(8,128)}) %reduce-scatter.7.cloned.1.call-update) | async-done | bytes 524304
  237.6 1.3 copy.22
  238.9 0.9 copy.20
  (2 shorter events, 0.1 us)
Async XLA Ops:
  7.2 94.4 %all-gather.3.cloned.1.call-start = ((), (), s32[]{:S(2)}) async-start(), calls=%async_computation.2 | async-start | bytes 2293760 | tf_op jit(solution)/shard_map/all_gather | solution.py:44
  7.9 118.8 %all-gather.5.cloned.1.call-start = ((), (), s32[]{:S(2)}) async-start(), calls=%async_computation.4 | async-start | bytes 2293760 | tf_op jit(solution)/shard_map/all_gather | solution.py:54
  8.6 154.5 %reduce-scatter.5.cloned.1.call-start = ((), (), s32[]{:S(2)}) async-start(), calls=%async_computation.3 | async-start | bytes 4587520 | tf_op jit(solution)/shard_map/reduce_scatter | solution.py:35
  11.7 3.1 %collective-permute-start = (bf16[128,2048]{1,0:T(8,128)(2,1)}, bf16[128,2048]{1,0:T(8,128)(2,1)}, u32[]{:S(2)}, u32[]{:S(2)}) collective-permute-start(bf16[128,2048]{1,0:T(8,128)(2,1)} %get-tuple-element.10), channel_id=1, source_target_pairs={{0,1},{1,0},{2,3},{3,2},{4,5},{5,4},{6,7},{7,6},{8,9},{9,8},{10,11... | collective-permute-start | bytes 1572872 | tf_op jit(solution)/shard_map/ppermute | solution.py:26
  12.2 22.1 %collective-permute-start.1 = (bf16[128,2048]{1,0:T(8,128)(2,1)}, bf16[128,2048]{1,0:T(8,128)(2,1)S(1)}, u32[]{:S(2)}, u32[]{:S(2)}) collective-permute-start(bf16[128,2048]{1,0:T(8,128)(2,1)} %get-tuple-element.12), channel_id=1, source_target_pairs={{0,2},{1,3},{2,0},{3,1},{4,6},{5,7},{6,4},{7,5},{8,10},{9,11},{10,... | collective-permute-start | bytes 1572872 | tf_op jit(solution)/shard_map/ppermute | solution.py:26
  14.7 33.7 %collective-permute-start.2 = (bf16[128,2048]{1,0:T(8,128)(2,1)}, bf16[128,2048]{1,0:T(8,128)(2,1)S(1)}, u32[]{:S(2)}, u32[]{:S(2)}) collective-permute-start(bf16[128,2048]{1,0:T(8,128)(2,1)} %get-tuple-element.9), channel_id=1, source_target_pairs={{0,3},{1,2},{2,1},{3,0},{4,7},{5,6},{6,5},{7,4},{8,11},{9,10},{10,... | collective-permute-start | bytes 1572872 | tf_op jit(solution)/shard_map/ppermute | solution.py:26
  58.1 179.5 %reduce-scatter.7.cloned.1.call-start = ((), (), s32[]{:S(2)}) async-start(), calls=%async_computation.5 | async-start | bytes 4718592
Sparse Core Ops, SparseCore 0:
  9.6 33.7 all-gather.2
  44.9 21.1 all-gather.4
  68.6 41.2 reduce-scatter.4
  148.1 89.4 reduce-scatter.6
